TPU v7x, 32 devices: a whole 2x2x4 slice. The times are simulated.
32 devices in a mesh: seq: 4 (over x, core), clip: 8 (over z, y).
Axes of the slice: x: 2, y: 2, z: 4, core: 2. Of those that a mesh axis runs over, the one named last changes fastest.
Arguments:
- x_vis: bfloat16 [24, 157, 768], P('clip'), may hold values from -6 to 6
- vis_pos: int32 [24, 157], P('clip'), may hold values from 0 to 1567, as said below
- w_proj: bfloat16 [768, 384], replicated, may hold values from -0.21875 to 0.21875
- b_proj: float32 [384], replicated, may hold values from -3 to 3
- mask_token: float32 [384], replicated, may hold values from -4 to 4
- ln1_gain: float32 [384], replicated, may hold values from 0.25 to 1.75
- ln1_bias: float32 [384], replicated, may hold values from -2 to 2
- w_qkv: bfloat16 [384, 1152], replicated, may hold values from -0.3125 to 0.3125
- q_bias: float32 [384], replicated, may hold values from -2 to 2
- v_bias: float32 [384], replicated, may hold values from -3 to 3
- w_out: bfloat16 [384, 384], replicated, may hold values from -4 to 4
- b_out: float32 [384], replicated, may hold values from -2 to 2
- ln2_gain: float32 [384], replicated, may hold values from 0.25 to 1.75
- ln2_bias: float32 [384], replicated, may hold values from -2 to 2
- w_fc1: bfloat16 [384, 1536], replicated, may hold values from -0.3125 to 0.3125
- b_fc1: float32 [1536], replicated, may hold values from -3 to 3
- w_fc2: bfloat16 [1536, 384], replicated, may hold values from -0.15625 to 0.15625
- b_fc2: float32 [384], replicated, may hold values from -2 to 2
- cotangent: bfloat16 [24, 1568, 384], P('clip', 'seq'), may hold values from -6 to 6
Outputs:
- output: bfloat16 [24, 1568, 384], P('clip', 'seq')
- grad_x: float32 [24, 157, 768], P('clip')
- grad_w_proj: float32 [768, 384], replicated
- grad_b_proj: float32 [384], replicated
- grad_mask: float32 [384], replicated
- grad_ln1_gain: float32 [384], replicated
- grad_ln1_bias: float32 [384], replicated
- grad_w_qkv: float32 [384, 1152], replicated
- grad_q_bias: float32 [384], replicated
- grad_v_bias: float32 [384], replicated
- grad_w_out: float32 [384, 384], replicated
- grad_b_out: float32 [384], replicated
- grad_ln2_gain: float32 [384], replicated
- grad_ln2_bias: float32 [384], replicated
- grad_w_fc1: float32 [384, 1536], replicated
- grad_b_fc1: float32 [1536], replicated
- grad_w_fc2: float32 [1536, 384], replicated
- grad_b_fc2: float32 [384], replicated
- trust: float32 [4], replicated
- trust_qkv: float32 [1], replicated
Inputs may be any that keep to these rules, and one draw needn't show every extreme that they name: `vis_pos`: each clip's 157 visible positions, in rising order, all different.
All inputs are finite; a program needn't handle non-finite values.
Results may differ from a plain program's by a relative error of at most 0.01.
Values may be sent and summed in bfloat16 or wider, within the bound.
No kernel may reach another device: no remote copies, remote signals or barrier semaphores. Data moves between devices by JAX's collectives and lax.ppermute only.
A program may use at most 256 MiB of HBM per device.

v0:
```python
import math
import jax
import jax.numpy as jnp
from jax import lax
from jax.sharding import PartitionSpec as P

D = 384
HEADS = 6
HEAD = 64
LEN = 1568
exact_prec = lax.Precision.HIGHEST


def sinusoid(length, columns):
    positions = jnp.arange(length, dtype=jnp.float32)[:, None]
    column = jnp.arange(columns, dtype=jnp.int32)
    exponent = (2 * (column // 2)).astype(jnp.float32) / columns
    angles = positions / jnp.power(10000.0, exponent)[None, :]
    return jnp.where((column % 2)[None, :] == 0, jnp.sin(angles), jnp.cos(angles))


def layer_norm(inputs, gain_vec, shift_vec):
    average = jnp.mean(inputs, axis=-1, keepdims=True)
    centered = inputs - average
    variance = jnp.mean(centered * centered, axis=-1, keepdims=True)
    return centered * lax.rsqrt(variance + 1e-05) * gain_vec + shift_vec


def gelu_exact(values):
    return jax.nn.gelu(values, approximate=False)


def shards(
    x_vis,
    vis_pos,
    w_proj,
    b_proj,
    mask_token,
    ln1_gain,
    ln1_bias,
    w_qkv,
    q_bias,
    v_bias,
    w_out,
    b_out,
    ln2_gain,
    ln2_bias,
    w_fc1,
    b_fc1,
    w_fc2,
    b_fc2,
    cotangent,
):
    row_count = LEN // lax.axis_size("seq")
    score_scale = HEAD ** (-0.5)
    first_row = lax.axis_index("seq") * row_count
    projected = (
        jnp.einsum("cvi,id->cvd", x_vis, w_proj, preferred_element_type=jnp.float32) + b_proj
    )
    places = first_row + lax.iota(jnp.int32, row_count)
    onehot = (vis_pos[:, None, :] == places[None, :, None]).astype(jnp.float32)
    visible = jnp.sum(onehot, axis=2, keepdims=True)
    position_table = lax.dynamic_slice_in_dim(sinusoid(LEN, D), first_row, row_count, 0)
    embedded = (
        jnp.einsum("crv,cvd->crd", onehot, projected, precision=exact_prec)
        + (1.0 - visible) * mask_token
        + position_table
    )
    normed = layer_norm(embedded, ln1_gain, ln1_bias).astype(jnp.bfloat16)
    qkv_mixed = jnp.einsum("crd,de->cre", normed, w_qkv, preferred_element_type=jnp.float32)
    queries = (qkv_mixed[..., :D] + q_bias).astype(jnp.bfloat16)
    keys_local = qkv_mixed[..., D : 2 * D].astype(jnp.bfloat16)
    values_local = (qkv_mixed[..., 2 * D :] + v_bias).astype(jnp.bfloat16)
    keys_all, values_all = (
        lax.all_gather(keys_local, "seq", axis=1, tiled=True),
        lax.all_gather(values_local, "seq", axis=1, tiled=True),
    )

    def attend(sliced):
        query_one, key_one, value_one = sliced
        q_heads = query_one.reshape(row_count, HEADS, HEAD)
        k_heads = key_one.reshape(LEN, HEADS, HEAD)
        v_heads = value_one.reshape(LEN, HEADS, HEAD)
        scores = (
            jnp.einsum("qhe,khe->hqk", q_heads, k_heads, preferred_element_type=jnp.float32)
            * score_scale
        )
        largest = jnp.max(scores, axis=-1, keepdims=True)
        exponent = jnp.exp(scores - largest)
        totals = jnp.sum(exponent, axis=-1, keepdims=True)
        attn_probs = (exponent / totals).astype(jnp.bfloat16)
        attended = jnp.einsum(
            "hqk,khe->qhe", attn_probs, v_heads, preferred_element_type=jnp.float32
        )
        return (attended.reshape(row_count, D).astype(jnp.bfloat16), largest + jnp.log(totals))

    attended, log_totals = lax.map(attend, (queries, keys_all, values_all))
    branch = jnp.einsum("crd,de->cre", attended, w_out, preferred_element_type=jnp.float32) + b_out
    middle = embedded + branch
    normed2 = layer_norm(middle, ln2_gain, ln2_bias).astype(jnp.bfloat16)
    hidden_pre = (
        jnp.einsum("crd,df->crf", normed2, w_fc1, preferred_element_type=jnp.float32) + b_fc1
    )
    hidden = gelu_exact(hidden_pre).astype(jnp.bfloat16)
    output = (
        middle
        + jnp.einsum("crf,fd->crd", hidden, w_fc2, preferred_element_type=jnp.float32)
        + b_fc2
    ).astype(jnp.bfloat16)
    grad_out_f = cotangent.astype(jnp.float32)
    grad_w_fc2 = jnp.einsum("crf,crd->fd", hidden, cotangent, preferred_element_type=jnp.float32)
    grad_b_fc2 = jnp.sum(grad_out_f, axis=(0, 1))
    grad_hidden = jnp.einsum("crd,fd->crf", cotangent, w_fc2, preferred_element_type=jnp.float32)
    unused_gelu, pull_gelu = jax.vjp(gelu_exact, hidden_pre)
    grad_pre = pull_gelu(grad_hidden)[0].astype(jnp.bfloat16)
    grad_w_fc1 = jnp.einsum("crd,crf->df", normed2, grad_pre, preferred_element_type=jnp.float32)
    grad_b_fc1 = jnp.sum(grad_pre.astype(jnp.float32), axis=(0, 1))
    grad_normed2 = jnp.einsum("crf,df->crd", grad_pre, w_fc1, preferred_element_type=jnp.float32)
    unused_norm2, pull_norm2 = jax.vjp(layer_norm, middle, ln2_gain, ln2_bias)
    grad_mid_ln, grad_ln2_gain, grad_ln2_bias = pull_norm2(grad_normed2)
    grad_middle = grad_out_f + grad_mid_ln
    grad_branch = grad_middle.astype(jnp.bfloat16)
    grad_w_out = jnp.einsum(
        "crd,cre->de", attended, grad_branch, preferred_element_type=jnp.float32
    )
    grad_b_out = jnp.sum(grad_branch.astype(jnp.float32), axis=(0, 1))
    grad_attended = jnp.einsum(
        "cre,de->crd", grad_branch, w_out, preferred_element_type=jnp.float32
    ).astype(jnp.bfloat16)

    def attend_back(sliced):
        query_one, key_one, value_one, grad_one, logtot_one = sliced
        q_heads = query_one.reshape(row_count, HEADS, HEAD)
        k_heads = key_one.reshape(LEN, HEADS, HEAD)
        v_heads = value_one.reshape(LEN, HEADS, HEAD)
        g_heads = grad_one.reshape(row_count, HEADS, HEAD)
        scores = (
            jnp.einsum("qhe,khe->hqk", q_heads, k_heads, preferred_element_type=jnp.float32)
            * score_scale
        )
        attn_probs = jnp.exp(scores - logtot_one)
        grad_probs = jnp.einsum(
            "qhe,khe->hqk", g_heads, v_heads, preferred_element_type=jnp.float32
        )
        row_inner = jnp.sum(grad_probs * attn_probs, axis=-1, keepdims=True)
        grad_scores = (attn_probs * (grad_probs - row_inner)).astype(jnp.bfloat16)
        grad_query = (
            jnp.einsum(
                "hqk,khe->qhe", grad_scores, k_heads, preferred_element_type=jnp.float32
            ).reshape(row_count, D)
            * score_scale
        )
        grad_key = (
            jnp.einsum(
                "hqk,qhe->khe", grad_scores, q_heads, preferred_element_type=jnp.float32
            ).reshape(LEN, D)
            * score_scale
        )
        grad_value = jnp.einsum(
            "hqk,qhe->khe",
            attn_probs.astype(jnp.bfloat16),
            g_heads,
            preferred_element_type=jnp.float32,
        ).reshape(LEN, D)
        return (grad_query, grad_key, grad_value)

    grad_query, grad_key_part, grad_value_part = lax.map(
        attend_back, (queries, keys_all, values_all, grad_attended, log_totals)
    )
    grad_keys, grad_values = (
        lax.psum_scatter(grad_key_part, "seq", scatter_dimension=1, tiled=True),
        lax.psum_scatter(grad_value_part, "seq", scatter_dimension=1, tiled=True),
    )
    grad_qkv = jnp.concatenate(
        [
            grad_query.astype(jnp.bfloat16),
            grad_keys.astype(jnp.bfloat16),
            grad_values.astype(jnp.bfloat16),
        ],
        axis=-1,
    )
    grad_q_bias = jnp.sum(grad_qkv[..., :D].astype(jnp.float32), axis=(0, 1))
    grad_v_bias = jnp.sum(grad_qkv[..., 2 * D :].astype(jnp.float32), axis=(0, 1))
    grad_w_qkv = jnp.einsum("crd,cre->de", normed, grad_qkv, preferred_element_type=jnp.float32)
    grad_normed = jnp.einsum("cre,de->crd", grad_qkv, w_qkv, preferred_element_type=jnp.float32)
    unused_norm1, pull_norm1 = jax.vjp(layer_norm, embedded, ln1_gain, ln1_bias)
    grad_emb_ln, grad_ln1_gain, grad_ln1_bias = pull_norm1(grad_normed)
    grad_embedded = grad_middle + grad_emb_ln
    grad_mask = jnp.sum(grad_embedded * (1.0 - visible), axis=(0, 1))
    grad_proj_part = jnp.einsum("crv,crd->cvd", onehot, grad_embedded, precision=exact_prec)
    grad_projected = lax.psum(grad_proj_part.astype(jnp.bfloat16), "seq")
    grad_x = jnp.einsum("cvd,id->cvi", grad_projected, w_proj, preferred_element_type=jnp.float32)
    leading = (lax.axis_index("seq") == 0).astype(jnp.float32)
    grad_w_proj = (
        jnp.einsum("cvi,cvd->id", x_vis, grad_projected, preferred_element_type=jnp.float32)
        * leading
    )
    grad_b_proj = jnp.sum(grad_projected.astype(jnp.float32), axis=(0, 1)) * leading
    grad_list = [
        grad_w_proj,
        grad_b_proj,
        grad_mask,
        grad_ln1_gain,
        grad_ln1_bias,
        grad_w_qkv,
        grad_q_bias,
        grad_v_bias,
        grad_w_out,
        grad_b_out,
        grad_ln2_gain,
        grad_ln2_bias,
        grad_w_fc1,
        grad_b_fc1,
        grad_w_fc2,
        grad_b_fc2,
    ]
    offsets = []
    running = 0
    for tensor in grad_list:
        offsets.append(running)
        running += math.prod(tensor.shape)
    flat = jnp.concatenate([tensor.reshape(-1) for tensor in grad_list])
    matrix_slots = [0, 5, 8, 12, 14]
    matrix_list = [w_proj, w_qkv, w_out, w_fc1, w_fc2]
    counts_list = [math.prod(grad_list[slot].shape) for slot in matrix_slots]
    summed = lax.psum(flat, ("seq", "clip"))
    squares = jnp.stack(
        [
            jnp.sum(summed[offsets[slot] : offsets[slot] + counts_list[number]] ** 2)
            for number, slot in enumerate(matrix_slots)
        ]
    )
    results = [
        summed[offsets[number] : offsets[number] + math.prod(tensor.shape)].reshape(tensor.shape)
        for number, tensor in enumerate(grad_list)
    ]
    trust_all = jnp.stack(
        [
            jnp.sqrt(jnp.mean(matrix.astype(jnp.float32) ** 2))
            / jnp.sqrt(squares[number] / counts_list[number] + 1e-06)
            for number, matrix in enumerate(matrix_list)
        ]
    )
    trust = jnp.concatenate([trust_all[:1], trust_all[2:]])
    trust_qkv = trust_all[1:2]
    return (
        output,
        grad_x,
        results[0],
        results[1],
        results[2],
        results[3],
        results[4],
        results[5],
        results[6],
        results[7],
        results[8],
        results[9],
        results[10],
        results[11],
        results[12],
        results[13],
        results[14],
        results[15],
        trust,
        trust_qkv,
    )


def solution(mesh):
    return jax.shard_map(
        shards,
        mesh=mesh,
        in_specs=(
            P("clip", None, None),
            P("clip", None),
            P(),
            P(),
            P(),
            P(),
            P(),
            P(),
            P(),
            P(),
            P(),
            P(),
            P(),
            P(),
            P(),
            P(),
            P(),
            P(),
            P("clip", "seq", None),
        ),
        out_specs=(
            P("clip", "seq", None),
            P("clip", None, None),
            P(),
            P(),
            P(),
            P(),
            P(),
            P(),
            P(),
            P(),
            P(),
            P(),
            P(),
            P(),
            P(),
            P(),
            P(),
            P(),
            P(),
            P(),
        ),
        check_vma=False,
    )
```

profile of v0, /device:TPU:0, one launch (start us, length us, event | category | flops | bytes accessed | tf_op | source)
XLA Modules:
  0.0 848.6 jit_solution(2511256565757544996)
XLA Ops:
  26.8 28.8 %all-gather.5.cloned.1.call-done = bf16[3,1568,384]{2,1,0:T(8,128)(2,1)} async-done(((bf16[3,392,384]{2,1,0:T(8,128)(2,1)}), bf16[3,1568,384]{2,1,0:T(8,128)(2,1)}) %all-gather.5.cloned.1.call-update) | async-done | bytes 3612688 | tf_op jit(solution)/shard_map/all_gather | solution.py:75
  61.9 27.0 %all-gather.3.cloned.1.call-done = bf16[3,1568,384]{2,1,0:T(8,128)(2,1)} async-done(((bf16[3,392,384]{2,1,0:T(8,128)(2,1)}), bf16[3,1568,384]{2,1,0:T(8,128)(2,1)}) %all-gather.3.cloned.1.call-update) | async-done | bytes 3612688 | tf_op jit(solution)/shard_map/all_gather | solution.py:76
  95.2 81.8 %while.26 = (s32[]{:T(128)}, bf16[3,392,384]{1,2,0:T(8,128)(2,1)}, f32[3,6,392,1]{2,1,3,0:T(8,128)S(1)}, bf16[3,1568,384]{1,2,0:T(8,128)(2,1)}, bf16[3,392,384]{...) while((s32[]{:T(128)}, bf16[3,392,384]{1,2,0:T(8,128)(2,1)}, f32[3,6,392,1]{2,1,3,0:T(8,128)S(1)}, ...), condition=%wide.region_6.7_spmd, body=%wide.region_3.6_spmd.sunk | while | flops 977451200 | bytes 53475364 | solution.py:97
  98.3 7.9 multiply_reduce_fusion.21
  106.2 8.2 fusion.120
  125.3 7.9 multiply_reduce_fusion.21
  133.2 8.2 fusion.120
  152.4 7.9 multiply_reduce_fusion.21
  160.3 8.2 fusion.120
  183.8 17.4 %multiply_convert_fusion.1 = (bf16[3,392,1536]{2,1,0:T(8,128)(2,1)}, f32[3,392,1536]{2,1,0:T(8,128)S(1)}) fusion(f32[3,392,1536]{2,1,0:T(8,128)S(1)} %get-tuple-element.221, f32[1536]{0:T(1024)S(1)} %copy-done.55, u8[392,1536]{1,0:T(8,128)(4,1)S(1)} %get-tuple-element.140, u8[392,1536]{1,0:T(8,128)(4,1)S(1)} %get-tuple-element.139), kind=kLoop, calls=%fused_computation.39 | loop fusion | flops 128249856 | bytes 19273728 | tf_op jit(solution)/shard_map/convert_element_type | solution.py:104
  214.0 159.5 %while.27 = (s32[]{:T(128)}, bf16[3,392,384]{2,1,0:T(8,128)(2,1)}, f32[3,1568,384]{2,1,0:T(8,128)}, f32[3,1568,384]{2,1,0:T(8,128)}, bf16[3,1568,384]{1,2,0:T(8,...) while((s32[]{:T(128)}, bf16[3,392,384]{2,1,0:T(8,128)(2,1)}, ...), condition=%wide.region_13.14_spmd, body=%wide.region_11.13_spmd.sunk | while | flops 2405435136 | bytes 276586112 | solution.py:167
  231.2 14.4 %multiply_reduce_fusion.22 = (f32[6,392]{1,0:T(8,128)S(1)}, f32[6,392,1568]{2,1,0:T(8,128)}) fusion(f32[6,392,1568]{2,1,0:T(8,128)} %copy-done.1, f32[6,392]{1,0:T(8,128)S(1)} %dynamic-slice_bitcast_fusion.2, bf16[392,6,64]{0,2,1:T(8,128)(2,1)} %bitcast.165, bf16[1568,6,64]{0,2,1:T(8,128)(2,1)S(1)} %bitcast.164), kind=kOutput, calls=%fused_computation.13.clone.1 | convolution fusion | flops 486805184 | bytes 31027584 | tf_op jit(solution)/shard_map/while/body/eval_jaxpr/qhe,khe->hqk/dot_general | solution.py:142
  246.0 7.6 multiply_convert_fusion.3
  284.3 14.4 %multiply_reduce_fusion.22 = (f32[6,392]{1,0:T(8,128)S(1)}, f32[6,392,1568]{2,1,0:T(8,128)}) fusion(f32[6,392,1568]{2,1,0:T(8,128)} %copy-done.1, f32[6,392]{1,0:T(8,128)S(1)} %dynamic-slice_bitcast_fusion.2, bf16[392,6,64]{0,2,1:T(8,128)(2,1)} %bitcast.165, bf16[1568,6,64]{0,2,1:T(8,128)(2,1)S(1)} %bitcast.164), kind=kOutput, calls=%fused_computation.13.clone.1 | convolution fusion | flops 486805184 | bytes 31027584 | tf_op jit(solution)/shard_map/while/body/eval_jaxpr/qhe,khe->hqk/dot_general | solution.py:142
  299.1 7.6 multiply_convert_fusion.3
  337.3 14.4 %multiply_reduce_fusion.22 = (f32[6,392]{1,0:T(8,128)S(1)}, f32[6,392,1568]{2,1,0:T(8,128)}) fusion(f32[6,392,1568]{2,1,0:T(8,128)} %copy-done.1, f32[6,392]{1,0:T(8,128)S(1)} %dynamic-slice_bitcast_fusion.2, bf16[392,6,64]{0,2,1:T(8,128)(2,1)} %bitcast.165, bf16[1568,6,64]{0,2,1:T(8,128)(2,1)S(1)} %bitcast.164), kind=kOutput, calls=%fused_computation.13.clone.1 | convolution fusion | flops 486805184 | bytes 31027584 | tf_op jit(solution)/shard_map/while/body/eval_jaxpr/qhe,khe->hqk/dot_general | solution.py:142
  352.1 7.6 multiply_convert_fusion.3
  399.9 38.5 %reduce-scatter.5.cloned.1.call-done = f32[3,392,384]{2,1,0:T(8,128)} async-done(((f32[3,1568,384]{2,1,0:T(8,128)}), f32[3,392,384]{2,1,0:T(8,128)}) %reduce-scatter.5.cloned.1.call-update) | async-done | bytes 1806352 | tf_op jit(solution)/shard_map/reduce_scatter | solution.py:172
  441.0 64.7 %reduce-scatter.3.cloned.1.call-done = f32[3,392,384]{2,1,0:T(8,128)} async-done(((f32[3,1568,384]{2,1,0:T(8,128)}), f32[3,392,384]{2,1,0:T(8,128)}) %reduce-scatter.3.cloned.1.call-update) | async-done | bytes 1806352 | tf_op jit(solution)/shard_map/reduce_scatter | solution.py:171
  522.6 25.4 %all-reduce.3.cloned.1.call-done = bf16[3,157,384]{2,1,0:T(8,128)(2,1)} async-done(((bf16[3,157,384]{2,1,0:T(8,128)(2,1)}), bf16[3,157,384]{2,1,0:T(8,128)(2,1)}) %all-reduce.3.cloned.1.call-update) | async-done | bytes 361744 | tf_op jit(solution)/shard_map/psum | solution.py:191
  563.3 15.5 %dynamic-update-slice.5 = f32[2069760]{0:T(1024)} dynamic-update-slice(f32[2069760]{0:T(1024)} %constant_dynamic-update-slice_fusion.12, f32[442368]{0:T(1024)S(1)} %reshape.290, s32[]{} %constant.199) | dynamic-update-slice | bytes 3538948
  587.6 21.3 %dynamic-update-slice.12 = f32[2069760]{0:T(1024)} dynamic-update-slice(f32[2069760]{0:T(1024)} %constant_dynamic-update-slice_fusion.6, f32[589824]{0:T(1024)} %reshape.292, s32[]{} %constant.206) | dynamic-update-slice | bytes 4718596
  610.2 20.1 %dynamic-update-slice.14 = f32[2069760]{0:T(1024)} dynamic-update-slice(f32[2069760]{0:T(1024)} %constant_dynamic-update-slice_fusion.5, f32[589824]{0:T(1024)S(1)} %copy-done.15, s32[]{} %constant.208) | dynamic-update-slice | bytes 4718596
  652.4 158.5 %all-reduce.5.cloned.1.call-done = f32[2069760]{0:T(1024)} async-done(((f32[2069760]{0:T(1024)}), f32[2069760]{0:T(1024)}) %all-reduce.5.cloned.1.call-update) | async-done | bytes 8279056 | tf_op jit(solution)/shard_map/psum | solution.py:226
  (319 shorter events, 292.7 us)
Async XLA Ops:
  7.2 48.3 %all-gather.5.cloned.1.call-start = ((), (), s32[]{:S(2)}) async-start(), calls=%async_computation.3 | async-start | bytes 4515840 | tf_op jit(solution)/shard_map/all_gather | solution.py:75
  21.5 67.4 %all-gather.3.cloned.1.call-start = ((), (), s32[]{:S(2)}) async-start(), calls=%async_computation.2 | async-start | bytes 4515840 | tf_op jit(solution)/shard_map/all_gather | solution.py:76
  24.8 413.6 %reduce-scatter.5.cloned.1.call-start = ((), (), s32[]{:S(2)}) async-start(), calls=%async_computation.5 | async-start | bytes 9031680 | tf_op jit(solution)/shard_map/reduce_scatter | solution.py:172
  95.2 81.8 %copy-start.7 = (f32[3,392,384]{2,1,0:T(8,128)S(1)}, f32[3,392,384]{2,1,0:T(8,128)}, u32[]{:S(2)}) copy-start(f32[3,392,384]{2,1,0:T(8,128)} %copy-done.6) | copy-start | bytes 5419012
  95.2 81.8 %copy-start.25 = (bf16[384,384]{1,0:T(8,128)(2,1)S(1)}, bf16[384,384]{1,0:T(8,128)(2,1)}, u32[]{:S(2)}) copy-start(bf16[384,384]{1,0:T(8,128)(2,1)} %param.33) | copy-start | bytes 884740
  95.2 81.8 %copy-start.60 = (f32[384]{0:T(512)S(1)}, f32[384]{0:T(512)}, u32[]{:S(2)}) copy-start(f32[384]{0:T(512)} %param.34) | copy-start | bytes 4612
  179.4 29.9 %copy-start.9 = (f32[3,392,384]{2,1,0:T(8,128)}, f32[3,392,384]{2,1,0:T(8,128)S(1)}, u32[]{:S(2)}) copy-start(f32[3,392,384]{2,1,0:T(8,128)S(1)} %get-tuple-element.220) | copy-start | bytes 5419012
  179.4 29.9 %copy-start.32 = (f32[3,392]{1,0:T(4,128)}, f32[3,392]{1,0:T(4,128)S(1)}, u32[]{:S(2)}) copy-start(f32[3,392]{1,0:T(4,128)S(1)} %broadcast_multiply_fusion) | copy-start | bytes 14116
  180.0 29.3 %copy-start.36 = (f32[3,392]{1,0:T(4,128)}, f32[3,392]{1,0:T(4,128)S(1)}, u32[]{:S(2)}) copy-start(f32[3,392]{1,0:T(4,128)S(1)} %fusion.51) | copy-start | bytes 14116
  183.8 17.4 %copy-start.18 = (bf16[3,392,384]{2,1,0:T(8,128)(2,1)S(1)}, bf16[3,392,384]{2,1,0:T(8,128)(2,1)}, u32[]{:S(2)}) copy-start(bf16[3,392,384]{2,1,0:T(8,128)(2,1)} %param.41) | copy-start | bytes 2709508
  183.8 17.4 %copy-start.30 = (bf16[1536,384]{1,0:T(8,128)(2,1)S(1)}, bf16[1536,384]{1,0:T(8,128)(2,1)}, u32[]{:S(2)}) copy-start(bf16[1536,384]{1,0:T(8,128)(2,1)} %param.39) | copy-start | bytes 3538948
  231.2 14.8 %copy-start.2 = (f32[6,392,1568]{2,1,0:T(8,128)S(1)}, f32[6,392,1568]{2,1,0:T(8,128)}, u32[]{:S(2)}) copy-start(f32[6,392,1568]{2,1,0:T(8,128)} %copy-done.1) | copy-start | bytes 44255236 | tf_op jit(solution)/shard_map/while
  337.3 14.8 %copy-start.2 = (f32[6,392,1568]{2,1,0:T(8,128)S(1)}, f32[6,392,1568]{2,1,0:T(8,128)}, u32[]{:S(2)}) copy-start(f32[6,392,1568]{2,1,0:T(8,128)} %copy-done.1) | copy-start | bytes 44255236 | tf_op jit(solution)/shard_map/while
  373.5 132.2 %reduce-scatter.3.cloned.1.call-start = ((), (), s32[]{:S(2)}) async-start(), calls=%async_computation.4 | async-start | bytes 9031680 | tf_op jit(solution)/shard_map/reduce_scatter | solution.py:171
  374.1 173.9 %all-reduce.3.cloned.1.call-start = ((), (), s32[]{:S(2)}) async-start(), calls=%async_computation.6 | async-start | bytes 737280 | tf_op jit(solution)/shard_map/psum | solution.py:191
  396.4 110.9 %copy-start.8 = (f32[3,392,384]{2,1,0:T(8,128)S(1)}, f32[3,392,384]{2,1,0:T(8,128)}, u32[]{:S(2)}) copy-start(f32[3,392,384]{2,1,0:T(8,128)} %copy-done.6) | copy-start | bytes 5419012
  396.4 110.9 %copy-start.35 = (f32[3,392]{1,0:T(4,128)S(1)}, f32[3,392]{1,0:T(4,128)}, u32[]{:S(2)}) copy-start(f32[3,392]{1,0:T(4,128)} %copy-done.34) | copy-start | bytes 14116
  396.4 110.9 %copy-start.54 = (f32[384]{0:T(512)S(1)}, f32[384]{0:T(512)}, u32[]{:S(2)}) copy-start(f32[384]{0:T(512)} %param.28) | copy-start | bytes 4612
  516.1 294.8 %all-reduce.5.cloned.1.call-start = ((), (), s32[]{:S(2)}) async-start(), calls=%async_computation.7 | async-start | bytes 16564224 | tf_op jit(solution)/shard_map/psum | solution.py:226
  555.5 28.2 %copy-start.56 = (f32[384]{0:T(512)S(1)}, f32[384]{0:T(512)}, u32[]{:S(2)}) copy-start(f32[384]{0:T(512)} %get-tuple-element.178) | copy-start | bytes 4612
  555.5 29.5 %copy-start.64 = (f32[384]{0:T(512)S(1)}, f32[384]{0:T(512)}, u32[]{:S(2)}) copy-start(f32[384]{0:T(512)} %get-tuple-element.143) | copy-start | bytes 4612
  555.5 30.8 %copy-start.63 = (f32[384]{0:T(512)S(1)}, f32[384]{0:T(512)}, u32[]{:S(2)}) copy-start(f32[384]{0:T(512)} %get-tuple-element.145) | copy-start | bytes 4612
  578.8 30.1 %copy-start.57 = (f32[1536]{0:T(1024)S(1)}, f32[1536]{0:T(1024)}, u32[]{:S(2)}) copy-start(f32[1536]{0:T(1024)} %get-tuple-element.224) | copy-start | bytes 18436
  578.8 31.4 %copy-start.15 = (f32[589824]{0:T(1024)S(1)}, f32[589824]{0:T(1024)}, u32[]{:S(2)}) copy-start(f32[589824]{0:T(1024)} %reshape.293) | copy-start | bytes 7077892
  (62 other events, 267.2 us)
Sparse Core Ops, SparseCore 0:
  21.6 33.8 all-gather.4
  57.7 31.1 all-gather.2
  373.6 64.7 reduce-scatter.4
  441.0 64.6 reduce-scatter.2
  516.2 31.7 all-reduce.2
  631.8 179.0 all-reduce.4
where the time goes:
time: 861 us; the launch traced here: 849 us
  waiting for transfers between devices  343 us (40%)
  local copies, waits for them, and re-layouts  193 us (22%)
  matrix products  181 us (21%)
  other arithmetic  106 us (12%)
  between operations  23.5 us (3%)
    psum x1, waiting for transfers between devices, shards(): summed = lax.psum(flat, ('seq', 'clip'))  158 us
    unnamed x132, local copies, waits for them, and re-layouts  79.6 us
    reduce_scatter x1, waiting for transfers between devices, shards(): lax.psum_scatter(grad_key_part, 'seq', scatter_dimension=1, tiled=True)  64.7 us
    dot_general x3, matrix products, attend_back(): jnp.einsum('qhe,khe->hqk', g_heads, v_heads, preferred_element_type=jnp.f...  43.3 us
    reduce_scatter x1, waiting for transfers between devices, shards(): lax.psum_scatter(grad_value_part, 'seq', scatter_dimension=1, tiled=True)  38.5 us
    dynamic_update_slice x15, local copies, waits for them, and re-layouts, shards(): lax.map(attend_back, (queries, keys_all, values_all, grad_attended, log_t...  36.6 us
    all_gather x1, waiting for transfers between devices, shards(): lax.all_gather(keys_local, 'seq', axis=1, tiled=True)  28.8 us
    all_gather x1, waiting for transfers between devices, shards(): lax.all_gather(values_local, 'seq', axis=1, tiled=True)  27 us
  transfers between devices with their start and end apart: 6, of which 6 were waited for; matrix products, arithmetic and copies ran while one was open for 7% of the time, Pallas kernels for 0%

commit v1 on v0

--- a/solution.py
+++ b/solution.py
@@ -9,6 +9,11 @@
 HEAD = 64
 LEN = 1568
 exact_prec = lax.Precision.HIGHEST
+
+
+def by_each_axis(x, inner_axis, outer_axis):
+    partial = lax.psum(x, inner_axis)
+    return lax.psum(partial, outer_axis)
 
 
 def sinusoid(length, columns):
@@ -223,7 +228,7 @@
     matrix_slots = [0, 5, 8, 12, 14]
     matrix_list = [w_proj, w_qkv, w_out, w_fc1, w_fc2]
     counts_list = [math.prod(grad_list[slot].shape) for slot in matrix_slots]
-    summed = lax.psum(flat, ("seq", "clip"))
+    summed = by_each_axis(flat, "clip", "seq")
     squares = jnp.stack(
         [
             jnp.sum(summed[offsets[slot] : offsets[slot] + counts_list[number]] ** 2)

time: 861 us -> 1100 us (1.28)
  waiting for transfers between devices: 343 us -> 586 us
    psum x1 -> x2, waiting for transfers between devices: 158 us -> 401 us  [the longest x1 268 us: by_each_axis(): partial = lax.psum(x, inner_axis)]
  transfers between devices with their start and end apart: 6 -> 7, of which waited for: 6 -> 7; matrix products, arithmetic and copies ran while one was open for 7% -> 6% of each run, Pallas kernels for 0% -> 0%
where the time goes in v1:
time: 1100 us; the launch traced here: 1090 us
  waiting for transfers between devices  586 us (53%)
  local copies, waits for them, and re-layouts  193 us (18%)
  matrix products  181 us (16%)
  other arithmetic  106 us (10%)
  between operations  23.5 us (2%)
    psum x1, waiting for transfers between devices, by_each_axis(): partial = lax.psum(x, inner_axis)  268 us
    psum x1, waiting for transfers between devices, by_each_axis(): return lax.psum(partial, outer_axis)  133 us
    unnamed x132, local copies, waits for them, and re-layouts  79.6 us
    reduce_scatter x1, waiting for transfers between devices, shards(): lax.psum_scatter(grad_key_part, 'seq', scatter_dimension=1, tiled=True)  64.7 us
    dot_general x3, matrix products, attend_back(): jnp.einsum('qhe,khe->hqk', g_heads, v_heads, preferred_element_type=jnp.f...  43.3 us
    reduce_scatter x1, waiting for transfers between devices, shards(): lax.psum_scatter(grad_value_part, 'seq', scatter_dimension=1, tiled=True)  38.5 us
    dynamic_update_slice x15, local copies, waits for them, and re-layouts, shards(): lax.map(attend_back, (queries, keys_all, values_all, grad_attended, log_t...  36.6 us
    all_gather x1, waiting for transfers between devices, shards(): lax.all_gather(keys_local, 'seq', axis=1, tiled=True)  28.8 us
  transfers between devices with their start and end apart: 7, of which 7 were waited for; matrix products, arithmetic and copies ran while one was open for 6% of the time, Pallas kernels for 0%

profile of v1, /device:TPU:0, one launch (start us, length us, event | category | flops | bytes accessed | tf_op | source)
XLA Modules:
  0.0 1091.5 jit_solution(6682455427097610238)
XLA Ops:
  26.8 28.8 %all-gather.5.cloned.1.call-done = bf16[3,1568,384]{2,1,0:T(8,128)(2,1)} async-done(((bf16[3,392,384]{2,1,0:T(8,128)(2,1)}), bf16[3,1568,384]{2,1,0:T(8,128)(2,1)}) %all-gather.5.cloned.1.call-update) | async-done | bytes 3612688 | tf_op jit(solution)/shard_map/all_gather | solution.py:80
  61.9 27.0 %all-gather.3.cloned.1.call-done = bf16[3,1568,384]{2,1,0:T(8,128)(2,1)} async-done(((bf16[3,392,384]{2,1,0:T(8,128)(2,1)}), bf16[3,1568,384]{2,1,0:T(8,128)(2,1)}) %all-gather.3.cloned.1.call-update) | async-done | bytes 3612688 | tf_op jit(solution)/shard_map/all_gather | solution.py:81
  95.2 81.8 %while.26 = (s32[]{:T(128)}, bf16[3,392,384]{1,2,0:T(8,128)(2,1)}, f32[3,6,392,1]{2,1,3,0:T(8,128)S(1)}, bf16[3,1568,384]{1,2,0:T(8,128)(2,1)}, bf16[3,392,384]{...) while((s32[]{:T(128)}, bf16[3,392,384]{1,2,0:T(8,128)(2,1)}, f32[3,6,392,1]{2,1,3,0:T(8,128)S(1)}, ...), condition=%wide.region_6.7_spmd, body=%wide.region_3.6_spmd.sunk | while | flops 977451200 | bytes 53475364 | solution.py:102
  98.3 7.9 multiply_reduce_fusion.21
  106.2 8.2 fusion.120
  125.3 7.9 multiply_reduce_fusion.21
  133.2 8.2 fusion.120
  152.4 7.9 multiply_reduce_fusion.21
  160.3 8.2 fusion.120
  183.8 17.4 %multiply_convert_fusion.1 = (bf16[3,392,1536]{2,1,0:T(8,128)(2,1)}, f32[3,392,1536]{2,1,0:T(8,128)S(1)}) fusion(f32[3,392,1536]{2,1,0:T(8,128)S(1)} %get-tuple-element.221, f32[1536]{0:T(1024)S(1)} %copy-done.55, u8[392,1536]{1,0:T(8,128)(4,1)S(1)} %get-tuple-element.140, u8[392,1536]{1,0:T(8,128)(4,1)S(1)} %get-tuple-element.139), kind=kLoop, calls=%fused_computation.39 | loop fusion | flops 128249856 | bytes 19273728 | tf_op jit(solution)/shard_map/convert_element_type | solution.py:109
  214.0 159.5 %while.27 = (s32[]{:T(128)}, bf16[3,392,384]{2,1,0:T(8,128)(2,1)}, f32[3,1568,384]{2,1,0:T(8,128)}, f32[3,1568,384]{2,1,0:T(8,128)}, bf16[3,1568,384]{1,2,0:T(8,...) while((s32[]{:T(128)}, bf16[3,392,384]{2,1,0:T(8,128)(2,1)}, ...), condition=%wide.region_13.14_spmd, body=%wide.region_11.13_spmd.sunk | while | flops 2405435136 | bytes 276586112 | solution.py:172
  231.2 14.4 %multiply_reduce_fusion.22 = (f32[6,392]{1,0:T(8,128)S(1)}, f32[6,392,1568]{2,1,0:T(8,128)}) fusion(f32[6,392,1568]{2,1,0:T(8,128)} %copy-done.1, f32[6,392]{1,0:T(8,128)S(1)} %dynamic-slice_bitcast_fusion.2, bf16[392,6,64]{0,2,1:T(8,128)(2,1)} %bitcast.165, bf16[1568,6,64]{0,2,1:T(8,128)(2,1)S(1)} %bitcast.164), kind=kOutput, calls=%fused_computation.13.clone.1 | convolution fusion | flops 486805184 | bytes 31027584 | tf_op jit(solution)/shard_map/while/body/eval_jaxpr/qhe,khe->hqk/dot_general | solution.py:147
  246.0 7.6 multiply_convert_fusion.3
  284.3 14.4 %multiply_reduce_fusion.22 = (f32[6,392]{1,0:T(8,128)S(1)}, f32[6,392,1568]{2,1,0:T(8,128)}) fusion(f32[6,392,1568]{2,1,0:T(8,128)} %copy-done.1, f32[6,392]{1,0:T(8,128)S(1)} %dynamic-slice_bitcast_fusion.2, bf16[392,6,64]{0,2,1:T(8,128)(2,1)} %bitcast.165, bf16[1568,6,64]{0,2,1:T(8,128)(2,1)S(1)} %bitcast.164), kind=kOutput, calls=%fused_computation.13.clone.1 | convolution fusion | flops 486805184 | bytes 31027584 | tf_op jit(solution)/shard_map/while/body/eval_jaxpr/qhe,khe->hqk/dot_general | solution.py:147
  299.1 7.6 multiply_convert_fusion.3
  337.3 14.4 %multiply_reduce_fusion.22 = (f32[6,392]{1,0:T(8,128)S(1)}, f32[6,392,1568]{2,1,0:T(8,128)}) fusion(f32[6,392,1568]{2,1,0:T(8,128)} %copy-done.1, f32[6,392]{1,0:T(8,128)S(1)} %dynamic-slice_bitcast_fusion.2, bf16[392,6,64]{0,2,1:T(8,128)(2,1)} %bitcast.165, bf16[1568,6,64]{0,2,1:T(8,128)(2,1)S(1)} %bitcast.164), kind=kOutput, calls=%fused_computation.13.clone.1 | convolution fusion | flops 486805184 | bytes 31027584 | tf_op jit(solution)/shard_map/while/body/eval_jaxpr/qhe,khe->hqk/dot_general | solution.py:147
  399.9 38.5 %reduce-scatter.5.cloned.1.call-done = f32[3,392,384]{2,1,0:T(8,128)} async-done(((f32[3,1568,384]{2,1,0:T(8,128)}), f32[3,392,384]{2,1,0:T(8,128)}) %reduce-scatter.5.cloned.1.call-update) | async-done | bytes 1806352 | tf_op jit(solution)/shard_map/reduce_scatter | solution.py:177
  441.0 64.7 %reduce-scatter.3.cloned.1.call-done = f32[3,392,384]{2,1,0:T(8,128)} async-done(((f32[3,1568,384]{2,1,0:T(8,128)}), f32[3,392,384]{2,1,0:T(8,128)}) %reduce-scatter.3.cloned.1.call-update) | async-done | bytes 1806352 | tf_op jit(solution)/shard_map/reduce_scatter | solution.py:176
  522.4 25.6 %all-reduce.4.cloned.1.call-done = bf16[3,157,384]{2,1,0:T(8,128)(2,1)} async-done(((bf16[3,157,384]{2,1,0:T(8,128)(2,1)}), bf16[3,157,384]{2,1,0:T(8,128)(2,1)}) %all-reduce.4.cloned.1.call-update) | async-done | bytes 361744 | tf_op jit(solution)/shard_map/psum | solution.py:196
  563.3 15.5 %dynamic-update-slice.5 = f32[2069760]{0:T(1024)} dynamic-update-slice(f32[2069760]{0:T(1024)} %constant_dynamic-update-slice_fusion.12, f32[442368]{0:T(1024)S(1)} %reshape.290, s32[]{} %constant.199) | dynamic-update-slice | bytes 3538948
  587.6 21.3 %dynamic-update-slice.12 = f32[2069760]{0:T(1024)} dynamic-update-slice(f32[2069760]{0:T(1024)} %constant_dynamic-update-slice_fusion.6, f32[589824]{0:T(1024)} %reshape.292, s32[]{} %constant.206) | dynamic-update-slice | bytes 4718596
  610.2 20.1 %dynamic-update-slice.14 = f32[2069760]{0:T(1024)} dynamic-update-slice(f32[2069760]{0:T(1024)} %constant_dynamic-update-slice_fusion.5, f32[589824]{0:T(1024)S(1)} %copy-done.15, s32[]{} %constant.208) | dynamic-update-slice | bytes 4718596
  631.9 268.5 %all-reduce.6.cloned.1.call-done = f32[2069760]{0:T(1024)} async-done(((f32[2069760]{0:T(1024)}), f32[2069760]{0:T(1024)}) %all-reduce.6.cloned.1.call-update) | async-done | bytes 8279056 | tf_op jit(solution)/shard_map/psum | solution.py:15
  921.0 132.7 %all-reduce.8.cloned.1.call-done = f32[2069760]{0:T(1024)} async-done(((f32[2069760]{0:T(1024)}), f32[2069760]{0:T(1024)}) %all-reduce.8.cloned.1.call-update) | async-done | bytes 8279056 | tf_op jit(solution)/shard_map/psum | solution.py:16
  (322 shorter events, 300.2 us)
Async XLA Ops:
  7.2 48.3 %all-gather.5.cloned.1.call-start = ((), (), s32[]{:S(2)}) async-start(), calls=%async_computation.3 | async-start | bytes 4515840 | tf_op jit(solution)/shard_map/all_gather | solution.py:80
  21.5 67.4 %all-gather.3.cloned.1.call-start = ((), (), s32[]{:S(2)}) async-start(), calls=%async_computation.2 | async-start | bytes 4515840 | tf_op jit(solution)/shard_map/all_gather | solution.py:81
  24.8 413.6 %reduce-scatter.5.cloned.1.call-start = ((), (), s32[]{:S(2)}) async-start(), calls=%async_computation.5 | async-start | bytes 9031680 | tf_op jit(solution)/shard_map/reduce_scatter | solution.py:177
  95.2 81.8 %copy-start.7 = (f32[3,392,384]{2,1,0:T(8,128)S(1)}, f32[3,392,384]{2,1,0:T(8,128)}, u32[]{:S(2)}) copy-start(f32[3,392,384]{2,1,0:T(8,128)} %copy-done.6) | copy-start | bytes 5419012
  95.2 81.8 %copy-start.25 = (bf16[384,384]{1,0:T(8,128)(2,1)S(1)}, bf16[384,384]{1,0:T(8,128)(2,1)}, u32[]{:S(2)}) copy-start(bf16[384,384]{1,0:T(8,128)(2,1)} %param.33) | copy-start | bytes 884740
  95.2 81.8 %copy-start.60 = (f32[384]{0:T(512)S(1)}, f32[384]{0:T(512)}, u32[]{:S(2)}) copy-start(f32[384]{0:T(512)} %param.34) | copy-start | bytes 4612
  179.4 29.9 %copy-start.9 = (f32[3,392,384]{2,1,0:T(8,128)}, f32[3,392,384]{2,1,0:T(8,128)S(1)}, u32[]{:S(2)}) copy-start(f32[3,392,384]{2,1,0:T(8,128)S(1)} %get-tuple-element.220) | copy-start | bytes 5419012
  179.4 29.9 %copy-start.32 = (f32[3,392]{1,0:T(4,128)}, f32[3,392]{1,0:T(4,128)S(1)}, u32[]{:S(2)}) copy-start(f32[3,392]{1,0:T(4,128)S(1)} %broadcast_multiply_fusion) | copy-start | bytes 14116
  180.0 29.3 %copy-start.36 = (f32[3,392]{1,0:T(4,128)}, f32[3,392]{1,0:T(4,128)S(1)}, u32[]{:S(2)}) copy-start(f32[3,392]{1,0:T(4,128)S(1)} %fusion.51) | copy-start | bytes 14116
  183.8 17.4 %copy-start.18 = (bf16[3,392,384]{2,1,0:T(8,128)(2,1)S(1)}, bf16[3,392,384]{2,1,0:T(8,128)(2,1)}, u32[]{:S(2)}) copy-start(bf16[3,392,384]{2,1,0:T(8,128)(2,1)} %param.41) | copy-start | bytes 2709508
  183.8 17.4 %copy-start.30 = (bf16[1536,384]{1,0:T(8,128)(2,1)S(1)}, bf16[1536,384]{1,0:T(8,128)(2,1)}, u32[]{:S(2)}) copy-start(bf16[1536,384]{1,0:T(8,128)(2,1)} %param.39) | copy-start | bytes 3538948
  231.2 14.8 %copy-start.2 = (f32[6,392,1568]{2,1,0:T(8,128)S(1)}, f32[6,392,1568]{2,1,0:T(8,128)}, u32[]{:S(2)}) copy-start(f32[6,392,1568]{2,1,0:T(8,128)} %copy-done.1) | copy-start | bytes 44255236 | tf_op jit(solution)/shard_map/while
  373.5 132.2 %reduce-scatter.3.cloned.1.call-start = ((), (), s32[]{:S(2)}) async-start(), calls=%async_computation.4 | async-start | bytes 9031680 | tf_op jit(solution)/shard_map/reduce_scatter | solution.py:176
  374.1 173.9 %all-reduce.4.cloned.1.call-start = ((), (), s32[]{:S(2)}) async-start(), calls=%async_computation.6 | async-start | bytes 737280 | tf_op jit(solution)/shard_map/psum | solution.py:196
  396.4 110.9 %copy-start.8 = (f32[3,392,384]{2,1,0:T(8,128)S(1)}, f32[3,392,384]{2,1,0:T(8,128)}, u32[]{:S(2)}) copy-start(f32[3,392,384]{2,1,0:T(8,128)} %copy-done.6) | copy-start | bytes 5419012
  396.4 110.9 %copy-start.35 = (f32[3,392]{1,0:T(4,128)S(1)}, f32[3,392]{1,0:T(4,128)}, u32[]{:S(2)}) copy-start(f32[3,392]{1,0:T(4,128)} %copy-done.34) | copy-start | bytes 14116
  396.4 110.9 %copy-start.54 = (f32[384]{0:T(512)S(1)}, f32[384]{0:T(512)}, u32[]{:S(2)}) copy-start(f32[384]{0:T(512)} %param.28) | copy-start | bytes 4612
  516.1 384.3 %all-reduce.6.cloned.1.call-start = ((), (), s32[]{:S(2)}) async-start(), calls=%async_computation.7 | async-start | bytes 16564224 | tf_op jit(solution)/shard_map/psum | solution.py:15
  555.5 28.2 %copy-start.56 = (f32[384]{0:T(512)S(1)}, f32[384]{0:T(512)}, u32[]{:S(2)}) copy-start(f32[384]{0:T(512)} %get-tuple-element.178) | copy-start | bytes 4612
  555.5 29.5 %copy-start.64 = (f32[384]{0:T(512)S(1)}, f32[384]{0:T(512)}, u32[]{:S(2)}) copy-start(f32[384]{0:T(512)} %get-tuple-element.143) | copy-start | bytes 4612
  555.5 30.8 %copy-start.63 = (f32[384]{0:T(512)S(1)}, f32[384]{0:T(512)}, u32[]{:S(2)}) copy-start(f32[384]{0:T(512)} %get-tuple-element.145) | copy-start | bytes 4612
  578.8 30.1 %copy-start.57 = (f32[1536]{0:T(1024)S(1)}, f32[1536]{0:T(1024)}, u32[]{:S(2)}) copy-start(f32[1536]{0:T(1024)} %get-tuple-element.224) | copy-start | bytes 18436
  578.8 31.4 %copy-start.15 = (f32[589824]{0:T(1024)S(1)}, f32[589824]{0:T(1024)}, u32[]{:S(2)}) copy-start(f32[589824]{0:T(1024)} %reshape.293) | copy-start | bytes 7077892
  631.6 422.2 %all-reduce.8.cloned.1.call-start = ((), (), s32[]{:S(2)}) async-start(), calls=%async_computation.8 | async-start | bytes 16564224 | tf_op jit(solution)/shard_map/psum | solution.py:16
  (63 other events, 281.5 us)
Sparse Core Ops, SparseCore 0:
  21.6 33.8 all-gather.4
  57.7 31.1 all-gather.2
  373.6 64.7 reduce-scatter.4
  441.0 64.6 reduce-scatter.2
  516.2 31.7 all-reduce.3
  631.7 268.6 all-reduce.5
  903.1 150.6 all-reduce.7
